TPU v7x, 32 devices: a whole 2x2x4 slice. The times are simulated.
32 devices in a mesh: group: 2 (over y), chan: 8 (over z, x), rec: 2 (over core).
Axes of the slice: x: 2, y: 2, z: 4, core: 2. Of those that a mesh axis runs over, the one named last changes fastest.
Arguments:
- records: bfloat16 [256, 128, 1024], P(('group', 'chan'), 'rec'), parts along dimension 0, may hold values from -50 to 50
- valid: int32 [256, 128], P(('group', 'chan'), 'rec'), parts along dimension 0, may hold values 0 or 1
- sources: int32 [16], P('group'), parts along dimension 0, may hold values from 0 to 127, as said below
Outputs:
- cross: float32 [256, 8, 1024], P(('group', 'chan'), None, 'rec'), parts along dimension 0
There are 2 independent parts, one for each index of `group`. A program takes and returns all parts, laid end to end along the dimension named above; each array names one. Nothing has to cross between parts.
Inputs may be any that keep to these rules, and one draw needn't show every extreme that they name: `sources`: 8 distinct channel numbers.
All inputs are finite; a program needn't handle non-finite values. No bound on the sum of `valid` on one device may be relied on, other than what follows from the above.
Results may differ from a plain program's by a relative error of at most 0.0034.
Values may be sent and summed in bfloat16 or wider, within the bound.
No kernel may reach another device: no remote copies, remote signals or barrier semaphores. Data moves between devices by JAX's collectives and lax.ppermute only.
A program may use at most 64 MiB of HBM per device.

v0:
```python
import functools
import math

import jax
import jax.numpy as jnp
import numpy as np
from jax import lax
from jax.experimental import pallas as pl
from jax.experimental.pallas import tpu as pltpu
from jax.sharding import PartitionSpec as P


VMEM = pl.BlockSpec(memory_space=pltpu.VMEM)
SMEM = pl.BlockSpec(memory_space=pltpu.SMEM)
LANES = 128
QUAD = 4
STREAMS = 2
ROOM = pltpu.CompilerParams(vmem_limit_bytes=16 << 20)


def dft_table(length, bins):
    times = np.arange(length)[:, None]
    freqs = np.arange(bins)[None, :]
    phase = (times * freqs % length) * (2.0 * math.pi / length)
    table = np.concatenate([np.cos(phase), -np.sin(phase)], axis=1)
    return jnp.asarray(table.astype(np.float32).astype(jnp.bfloat16))


def row_mask(valid_row, start, rows):
    n = valid_row.shape[1]
    lane = lax.broadcasted_iota(jnp.int32, (rows, n), 1)
    row = lax.broadcasted_iota(jnp.int32, (rows, n), 0)
    hit = jnp.where(lane == row + start, valid_row.astype(jnp.float32), 0.0)
    return jnp.sum(hit, axis=1, keepdims=True)


def owner_of(sources, per_dev, s):
    owner = sources[s] // per_dev
    rank = jnp.int32(0)
    for before in range(s):
        rank += (sources[before] // per_dev == owner).astype(jnp.int32)
    return owner, rank


def pick_kernel(sources, valid, records, *rest):
    outs, (which, usable, buf, sems) = rest[: 2 * QUAD], rest[2 * QUAD :]
    per_dev, rec_rows, _ = records.shape
    n_src = sources.shape[0]
    room = outs[0].shape[0]
    block = rec_rows // QUAD
    me = lax.axis_index("chan")
    quad = lax.rem(me, QUAD)
    get_sources = pltpu.make_async_copy(sources, which, sems.at[n_src])
    get_valid = pltpu.make_async_copy(valid, usable, sems.at[n_src + 1])
    get_sources.start()
    get_valid.start()
    get_sources.wait()

    def copy(s):
        local = which[s] - me * per_dev
        return pltpu.make_async_copy(records.at[local], buf.at[s], sems.at[s])

    for s in range(n_src):

        @pl.when(owner_of(which, per_dev, s)[0] == me)
        def _():
            copy(s).start()

    get_valid.wait()
    for s in range(n_src):
        owner, rank = owner_of(which, per_dev, s)

        @pl.when(owner == me)
        def _():
            copy(s).wait()
            row = usable[pl.ds(which[s] - me * per_dev, 1), :]
            for other in range(QUAD):
                start = pl.multiple_of((quad ^ other) * block, block)
                rows = buf[s, pl.ds(start, block), :].astype(jnp.float32)
                rows = (rows * row_mask(row, start, block)).astype(buf.dtype)

                @pl.when(rank < room)
                def _():
                    outs[other][jnp.minimum(rank, room - 1)] = rows

                @pl.when(rank >= room)
                def _():
                    outs[QUAD + other][jnp.maximum(rank - room, 0)] = rows


def pick(sources, valid, records, room):
    n_src = sources.shape[0]
    _, rec_rows, length = records.shape
    parts = [
        jax.ShapeDtypeStruct((count, rec_rows // QUAD, length), records.dtype)
        for count in (room, n_src - room)
    ]
    args = [pltpu.with_memory_space_constraint(x, pltpu.HBM) for x in (sources, valid, records)]
    return pl.pallas_call(
        pick_kernel,
        out_shape=(parts[0],) * QUAD + (parts[1],) * QUAD,
        in_specs=[pl.BlockSpec(memory_space=pltpu.HBM)] * 3,
        out_specs=(VMEM,) * (2 * QUAD),
        scratch_shapes=[
            pltpu.SMEM(sources.shape, sources.dtype),
            pltpu.VMEM(valid.shape, valid.dtype),
            pltpu.VMEM((n_src, rec_rows, length), records.dtype),
            pltpu.SemaphoreType.DMA((n_src + 2,)),
        ],
        compiler_params=ROOM,
        name="pick",
    )(*args)


def merge_kernel(per_dev, sources, *refs):
    firsts, others, outs = refs[:QUAD], refs[QUAD : 2 * QUAD], refs[2 * QUAD :]
    room = firsts[0].shape[0]
    part = outs[0].shape[1]
    me = lax.axis_index("chan")
    for s in range(sources.shape[0]):
        owner, rank = owner_of(sources, per_dev, s)
        near = owner // QUAD == me // QUAD

        def put(rows):
            for t, out in enumerate(outs):
                out[s] = rows[t * part : (t + 1) * part]

        @pl.when(jnp.logical_not(near))
        def _():
            for out in outs:
                out[s] = jnp.zeros(out.shape[1:], out.dtype)

        for j in range(QUAD):
            here = jnp.logical_and(near, lax.rem(owner, QUAD) ^ lax.rem(me, QUAD) == j)

            @pl.when(jnp.logical_and(here, rank < room))
            def _():
                put(firsts[j][jnp.minimum(rank, room - 1)])

            @pl.when(jnp.logical_and(here, rank >= room))
            def _():
                put(others[j][jnp.maximum(rank - room, 0)])


def merge(sources, per_dev, firsts, others):
    n_src = sources.shape[0]
    _, block, length = firsts[0].shape
    part = jax.ShapeDtypeStruct((n_src, block // STREAMS, length), firsts[0].dtype)
    return pl.pallas_call(
        functools.partial(merge_kernel, per_dev),
        out_shape=(part,) * STREAMS,
        in_specs=[SMEM] + [VMEM] * (2 * QUAD),
        out_specs=(VMEM,) * STREAMS,
        compiler_params=ROOM,
        name="merge",
    )(sources, *firsts, *others)


def spectra_kernel(chans, valid, table, records, out, buf, sems):
    per_dev, rec_rows, length = records.shape

    def copy(c0):
        part = pl.ds(c0, chans)
        return pltpu.make_async_copy(records.at[part], buf.at[part], sems.at[c0 // chans])

    for c0 in range(0, min(2 * chans, per_dev), chans):
        copy(c0).start()
    for c0 in range(0, per_dev, chans):
        copy(c0).wait()
        if c0 + 2 * chans < per_dev:
            copy(c0 + 2 * chans).start()
        flat = buf[c0 : c0 + chans].reshape(chans * rec_rows, length)
        spec = jnp.dot(flat, table[...], preferred_element_type=jnp.float32)
        for c in range(chans):
            mask = row_mask(valid[c0 + c : c0 + c + 1, :], 0, rec_rows)
            part = spec[c * rec_rows : (c + 1) * rec_rows] * mask
            for f in range(out.shape[0]):
                out[f, c0 + c] = part[:, f * LANES : (f + 1) * LANES]


def spectra_of(valid, table, records):
    per_dev, rec_rows, length = records.shape
    width = table.shape[1]
    chans = math.gcd(per_dev, 4)
    records = pltpu.with_memory_space_constraint(records, pltpu.HBM)
    return pl.pallas_call(
        functools.partial(spectra_kernel, chans),
        out_shape=jax.ShapeDtypeStruct((width // LANES, per_dev, rec_rows, LANES), jnp.float32),
        in_specs=[VMEM, VMEM, pl.BlockSpec(memory_space=pltpu.HBM)],
        out_specs=VMEM,
        scratch_shapes=[
            pltpu.VMEM(records.shape, records.dtype),
            pltpu.SemaphoreType.DMA((per_dev // chans,)),
        ],
        cost_estimate=pl.CostEstimate(
            flops=2 * per_dev * rec_rows * length * width,
            bytes_accessed=per_dev * rec_rows * (2 * length + 4 * width),
            transcendentals=0,
        ),
        compiler_params=ROOM,
        name="spectra",
    )(valid, table, records)


def whiten_kernel(table, mine, other, out, mixed):
    n_src, block, length = mine.shape
    bins = table.shape[1] // 2
    rows = (mine[...] + other[...]).reshape(n_src * block, length)
    spec = jnp.dot(rows, table[...], preferred_element_type=jnp.float32)
    real, imag = spec[:, :bins], spec[:, bins:]
    power = jnp.sum(real * real + imag * imag, axis=1, keepdims=True) / bins
    white = spec * lax.rsqrt(power + 1e-06)
    for f in range(0, 2 * bins, LANES):
        for s in range(n_src):
            part = white[s * block : (s + 1) * block, f : f + LANES]
            mixed[f // LANES, pl.ds(s, block, stride=n_src), :] = part
        out[:, f : f + LANES] = mixed[f // LANES].astype(out.dtype)


def whitened_of(table, mine, other):
    n_src, block, _ = mine.shape
    width = table.shape[1]
    rows = n_src * block
    return pl.pallas_call(
        whiten_kernel,
        out_shape=jax.ShapeDtypeStruct((rows, width), jnp.bfloat16),
        in_specs=[VMEM, VMEM, VMEM],
        out_specs=VMEM,
        scratch_shapes=[pltpu.VMEM((width // LANES, rows, LANES), jnp.float32)],
        compiler_params=ROOM,
        name="whiten",
    )(table, mine, other)


def cross_kernel(places, mode, first, spectra, *rest):
    both = mode == "both"
    whites, rest = rest[: len(places)], rest[len(places) :]
    acc, out, conj = (None, *rest) if first else rest
    chans, rec_rows = spectra.shape[1:3]
    width = whites[0].shape[1]
    n_src = out.shape[-2]
    part_rows = rec_rows // (QUAD * STREAMS)
    bins = width // 2
    tiles = bins // LANES
    quad = lax.rem(lax.axis_index("chan"), QUAD)
    core = lax.axis_index("rec")
    part = core if mode == "keep" else 1 - core
    for k, white in enumerate(whites):
        for f in range(tiles):
            real = white[:, f * LANES : (f + 1) * LANES].astype(jnp.float32)
            imag = white[:, bins + f * LANES : bins + (f + 1) * LANES].astype(jnp.float32)
            conj[k, 0, f] = real if both else jnp.where(part == 0, real, -imag)
            conj[k, 1, f] = imag if both else jnp.where(part == 0, imag, real)
    group = 8 if both else chans

    @pl.loop(0, tiles)
    def _(f):
        lo = pl.multiple_of(f * LANES, LANES)
        for c0 in range(0, chans, group):
            names = range(c0, c0 + group)
            if both:
                spots = [(p, c) for c in names for p in (0, 1)]
            else:
                spots = [(part, c) for c in names]
            if first:
                sums = [jnp.zeros((n_src, LANES), jnp.float32) for _ in spots]
            else:
                sums = [acc[p, c, :, pl.ds(lo, LANES)] for p, c in spots]
            for k, (other, stream) in enumerate(places):
                base = ((quad ^ other) * STREAMS + stream) * part_rows
                for r in range(part_rows):
                    a = conj[k, 0, f, r * n_src : (r + 1) * n_src, :]
                    b = conj[k, 1, f, r * n_src : (r + 1) * n_src, :]
                    for i, c in enumerate(names):
                        xr = spectra[f, c, pl.ds(base + r, 1), :]
                        xi = spectra[tiles + f, c, pl.ds(base + r, 1), :]
                        if both:
                            sums[2 * i] += xr * a + xi * b
                            sums[2 * i + 1] += xi * a - xr * b
                        else:
                            sums[i] += xr * a + xi * b
            for (p, c), total in zip(spots, sums):
                if both:
                    out[p, c, :, pl.ds(lo, LANES)] = total
                else:
                    out[c, :, pl.ds(lo, LANES)] = total.astype(out.dtype)


def cross_of(spectra, blocks, n_src, mode="both", acc=None):
    places, whites = zip(*blocks)
    chans = spectra.shape[1]
    rows, width = whites[0].shape
    bins = width // 2
    both = mode == "both"
    shape = (2, chans, n_src, bins) if both else (chans, n_src, bins)
    args = (spectra, *whites) + (() if acc is None else (acc,))
    return pl.pallas_call(
        functools.partial(cross_kernel, places, mode, acc is None),
        out_shape=jax.ShapeDtypeStruct(shape, jnp.bfloat16 if mode == "send" else jnp.float32),
        in_specs=[VMEM] * len(args),
        out_specs=VMEM,
        scratch_shapes=[pltpu.VMEM((len(places), 2, bins // LANES, rows, LANES), jnp.float32)],
        input_output_aliases={len(args) - 1: 0} if both and acc is not None else {},
        cost_estimate=pl.CostEstimate(
            flops=4 * (2 if both else 1) * chans * rows * bins * len(places) * 16,
            bytes_accessed=rows * chans * width * len(places),
            transcendentals=0,
        ),
        compiler_params=ROOM,
    )(*args)


def stacks(records, valid, sources):
    per_dev, rec_rows, length = records.shape
    bins = length // 2
    n_src = sources.shape[0]
    n_chan = lax.axis_size("chan")
    n_rec = lax.axis_size("rec")
    table = dft_table(length, bins)

    def swap(value, bit):
        return lax.ppermute(value, "chan", [(i, i ^ bit) for i in range(n_chan)])

    room = n_src // 2
    picked = pick(sources, valid, records, room)
    first, more = picked[:QUAD], picked[QUAD:]
    came = {j: swap(first[j], j) for j in (3, 1, 2)}
    owners = sources // per_dev
    held = jnp.sum(owners[:, None] == owners[None, :], axis=1)

    def scatter_more(parts):
        return [lax.ppermute(x, "chan", [(i, i ^ (j + 1)) for i in range(n_chan)]) for j, x in enumerate(parts)]

    rest = lax.cond(jnp.max(held) > room, scatter_more, lambda parts: parts, list(more[1:]))
    parts = merge(sources, per_dev, [first[0], came[1], came[2], came[3]], [more[0], *rest])
    last = n_chan // 2
    homes = []
    for t in range(STREAMS):
        home = parts[t]
        bit = QUAD
        while bit < last:
            home = home + swap(home, bit)
            bit *= 2
        homes.append((home, swap(home, last)))
    spectra = spectra_of(valid, table, records)
    acc = None
    gathered = []
    for t in range(STREAMS):
        home, other = homes[t]
        white = whitened_of(table, home, other)
        blocks = [((0, t), white)]
        for j in (3, 1, 2):
            blocks.append(((j, t), swap(white, j)))
        gathered.append(blocks)
        acc = cross_of(spectra, gathered[t][:1], n_src, "both", acc)
    for t in range(STREAMS):
        mine, *near, far = gathered[t]
        for block in near:
            acc = cross_of(spectra, [block], n_src, "both", acc)
        if t < STREAMS - 1:
            acc = cross_of(spectra, [far], n_src, "both", acc)
    send = cross_of(spectra, [far], n_src, "send", acc)
    came = lax.ppermute(send, "rec", [(i, i ^ 1) for i in range(n_rec)])
    keep = cross_of(spectra, [far], n_src, "keep", acc)
    return (keep + came.astype(jnp.float32)) / (rec_rows * n_rec)


def solution(mesh):
    placed = (P(("group", "chan"), "rec", None), P(("group", "chan"), "rec"), P("group"))
    return jax.shard_map(
        stacks,
        mesh=mesh,
        in_specs=placed,
        out_specs=P(("group", "chan"), None, "rec"),
        check_vma=False,
    )
```

profile of v0, /device:TPU:0, one launch (start us, length us, event | category | flops | bytes accessed | tf_op | source)
XLA Modules:
  0.0 46.1 jit_solution(3773395905222959020)
XLA Ops:
  0.0 2.2 %pick.1 = (bf16[4,16,1024]{2,1,0:T(8,128)(2,1)S(1)}, bf16[4,16,1024]{2,1,0:T(8,128)(2,1)S(1)}, bf16[4,16,1024]{2,1,0:T(8,128)(2,1)S(1)}, bf16[4,16,1024]{2,1,0:T...) custom-call(s32[8]{0:T(128)} %sources.3, ...), custom_call_target="tpu_custom_call" | custom-call | tf_op jit(solution)/shard_map/pick/pallas_call | solution.py:99
  2.2 3.0 %collective-permute-start.3 = (bf16[4,16,1024]{2,1,0:T(8,128)(2,1)S(1)}, bf16[4,16,1024]{2,1,0:T(8,128)(2,1)S(1)}, u32[]{:S(2)}, u32[]{:S(2)}) collective-permute-start(bf16[4,16,1024]{2,1,0:T(8,128)(2,1)S(1)} %get-tuple-element.34), channel_id=1, source_target_pairs={{0,2},{2,0},{4,6},{6,4},{8,10},{10,8},{12,14},{14,12},{1,3},{3,1},... | collective-permute-start | bytes 393224 | tf_op jit(solution)/shard_map/ppermute | solution.py:322
  5.2 1.5 %collective-permute-start.4 = (bf16[4,16,1024]{2,1,0:T(8,128)(2,1)S(1)}, bf16[4,16,1024]{2,1,0:T(8,128)(2,1)S(1)}, u32[]{:S(2)}, u32[]{:S(2)}) collective-permute-start(bf16[4,16,1024]{2,1,0:T(8,128)(2,1)S(1)} %get-tuple-element.35), channel_id=1, source_target_pairs={{0,4},{2,6},{4,0},{6,2},{8,12},{10,14},{12,8},{14,10},{1,5},{3,7},... | collective-permute-start | bytes 393224 | tf_op jit(solution)/shard_map/ppermute | solution.py:322
  6.7 0.2 convert_reduce_fusion
  6.9 0.6 %reduce_max.9 = s32[]{:T(128)} reduce(s32[8]{0:T(128)S(1)} %convert_reduce_fusion, s32[]{:T(128)} %constant.23.clone.1), dimensions={0}, to_apply=%region_1.2 | reduce | flops 7 | bytes 40 | tf_op jit(solution)/shard_map/reduce_max | solution.py:334
  8.3 0.3 collective-permute-done.3.refs_1_
  8.7 1.7 %collective-permute-done.4.refs_2_ = bf16[4,16,1024]{2,1,0:T(8,128)(2,1)S(1)} collective-permute-done((bf16[4,16,1024]{2,1,0:T(8,128)(2,1)S(1)}, bf16[4,16,1024]{2,1,0:T(8,128)(2,1)S(1)}, u32[]{:S(2)}, u32[]{:S(2)}) %collective-permute-start.4) | collective-permute-done | bytes 131104 | tf_op jit(solution)/shard_map/ppermute | solution.py:322
  10.4 3.7 %collective-permute-done.5.refs_3_ = bf16[4,16,1024]{2,1,0:T(8,128)(2,1)S(1)} collective-permute-done((bf16[4,16,1024]{2,1,0:T(8,128)(2,1)S(1)}, bf16[4,16,1024]{2,1,0:T(8,128)(2,1)S(1)}, u32[]{:S(2)}, u32[]{:S(2)}) %collective-permute-start.5) | collective-permute-done | bytes 131104 | tf_op jit(solution)/shard_map/ppermute | solution.py:322
  14.2 1.1 %merge.1 = (bf16[8,8,1024]{2,1,0:T(8,128)(2,1)S(1)}, bf16[8,8,1024]{2,1,0:T(8,128)(2,1)S(1)}) custom-call(s32[8]{0:T(128)S(1)} %copy-done.2, bf16[4,16,1024]{2,1,0:T(8,128)(2,1)S(1)} %get-tuple-element.33.refs_0_, bf16[4,16,1024]{2,1,0:T(8,128)(2,1)S(1)} %collective-permute-done.3.refs_1_, bf16[4,16,1024]{2,1,0:T(8,128)(2,1)S(1)} %collective-permute-done.4.refs_2_, ...), custom_call_target="tpu_custom_call" | custom-call | tf_op jit(solution)/shard_map/merge/pallas_call | solution.py:149
  15.3 2.7 %collective-permute-start.10 = (bf16[8,8,1024]{2,1,0:T(8,128)(2,1)S(1)}, bf16[8,8,1024]{2,1,0:T(8,128)(2,1)S(1)}, u32[]{:S(2)}, u32[]{:S(2)}) collective-permute-start(bf16[8,8,1024]{2,1,0:T(8,128)(2,1)S(1)} %get-tuple-element.45.mine), channel_id=1, source_target_pairs={{0,8},{2,10},{4,12},{6,14},{8,0},{10,2},{12,4},{14,6},{1,9},{3,11}... | collective-permute-start | bytes 393224 | tf_op jit(solution)/shard_map/ppermute | solution.py:322
  18.0 0.3 collective-permute-start.6
  18.3 8.5 %collective-permute-done.10.other = bf16[8,8,1024]{2,1,0:T(8,128)(2,1)S(1)} collective-permute-done((bf16[8,8,1024]{2,1,0:T(8,128)(2,1)S(1)}, bf16[8,8,1024]{2,1,0:T(8,128)(2,1)S(1)}, u32[]{:S(2)}, u32[]{:S(2)}) %collective-permute-start.10) | collective-permute-done | bytes 131104 | tf_op jit(solution)/shard_map/ppermute | solution.py:322
  26.8 0.6 %whiten.3.rest_0_ = bf16[64,1024]{1,0:T(8,128)(2,1)S(1)} custom-call(bf16[1024,1024]{1,0:T(8,128)(2,1)S(1)} %copy-done, bf16[8,8,1024]{2,1,0:T(8,128)(2,1)S(1)} %get-tuple-element.45.mine, bf16[8,8,1024]{2,1,0:T(8,128)(2,1)S(1)} %collective-permute-done.10.other), custom_call_target="tpu_custom_call" | custom-call | tf_op jit(solution)/shard_map/whiten/pallas_call | solution.py:224
  27.6 0.9 %collective-permute-start.12 = (bf16[64,1024]{1,0:T(8,128)(2,1)S(1)}, bf16[64,1024]{1,0:T(8,128)(2,1)S(1)}, u32[]{:S(2)}, u32[]{:S(2)}) collective-permute-start(bf16[64,1024]{1,0:T(8,128)(2,1)S(1)} %whiten.3.rest_0_), channel_id=1, source_target_pairs={{0,2},{2,0},{4,6},{6,4},{8,10},{10,8},{12,14},{14,12},{1,3},{3,1},... | collective-permute-start | bytes 393224 | tf_op jit(solution)/shard_map/ppermute | solution.py:322
  28.4 2.6 %collective-permute-start.11 = (bf16[64,1024]{1,0:T(8,128)(2,1)S(1)}, bf16[64,1024]{1,0:T(8,128)(2,1)S(1)}, u32[]{:S(2)}, u32[]{:S(2)}) collective-permute-start(bf16[64,1024]{1,0:T(8,128)(2,1)S(1)} %whiten.3.rest_0_), channel_id=1, source_target_pairs={{0,4},{2,6},{4,0},{6,2},{8,12},{10,14},{12,8},{14,10},{1,5},{3,7},... | collective-permute-start | bytes 393224 | tf_op jit(solution)/shard_map/ppermute | solution.py:322
  31.0 0.6 %whiten.2.rest_0_ = bf16[64,1024]{1,0:T(8,128)(2,1)S(1)} custom-call(bf16[1024,1024]{1,0:T(8,128)(2,1)S(1)} %copy-done, bf16[8,8,1024]{2,1,0:T(8,128)(2,1)S(1)} %get-tuple-element.44.mine, bf16[8,8,1024]{2,1,0:T(8,128)(2,1)S(1)} %collective-permute-done.6.other), custom_call_target="tpu_custom_call" | custom-call | tf_op jit(solution)/shard_map/whiten/pallas_call | solution.py:224
  31.7 0.3 collective-permute-start.9
  32.0 1.2 %collective-permute-start.8 = (bf16[64,1024]{1,0:T(8,128)(2,1)S(1)}, bf16[64,1024]{1,0:T(8,128)(2,1)S(1)}, u32[]{:S(2)}, u32[]{:S(2)}) collective-permute-start(bf16[64,1024]{1,0:T(8,128)(2,1)S(1)} %whiten.2.rest_0_), channel_id=1, source_target_pairs={{0,2},{2,0},{4,6},{6,4},{8,10},{10,8},{12,14},{14,12},{1,3},{3,1},... | collective-permute-start | bytes 393224 | tf_op jit(solution)/shard_map/ppermute | solution.py:322
  33.2 1.7 %collective-permute-done.13.rest_0_ = bf16[64,1024]{1,0:T(8,128)(2,1)S(1)} collective-permute-done((bf16[64,1024]{1,0:T(8,128)(2,1)S(1)}, bf16[64,1024]{1,0:T(8,128)(2,1)S(1)}, u32[]{:S(2)}, u32[]{:S(2)}) %collective-permute-start.13) | collective-permute-done | bytes 131104 | tf_op jit(solution)/shard_map/ppermute | solution.py:322
  34.9 0.3 collective-permute-start.7
  35.2 3.9 %spectra.1 = f32[8,16,64,128]{3,2,1,0:T(8,128)S(1)} custom-call(s32[16,64]{1,0:T(8,128)S(1)} %copy-done.1, bf16[1024,1024]{1,0:T(8,128)(2,1)S(1)} %copy-done, bf16[16,64,1024]{2,1,0:T(8,128)(2,1)} %records.3), custom_call_target="tpu_custom_call" | custom-call | flops 2147483648 | bytes 6291456 | tf_op jit(solution)/shard_map/spectra/pallas_call | solution.py:186
  39.2 0.6 %shard_map.46.rest_1_ = f32[2,16,8,512]{3,2,1,0:T(8,128)S(1)} custom-call(f32[8,16,64,128]{3,2,1,0:T(8,128)S(1)} %spectra.1, bf16[64,1024]{1,0:T(8,128)(2,1)S(1)} %whiten.3.rest_0_), custom_call_target="tpu_custom_call" | custom-call | flops 67108864 | bytes 1048576 | tf_op jit(solution)/shard_map/pallas_call | solution.py:297
  39.7 0.6 %shard_map.47.rest_1_ = f32[2,16,8,512]{3,2,1,0:T(8,128)S(1)} custom-call(f32[8,16,64,128]{3,2,1,0:T(8,128)S(1)} %spectra.1, bf16[64,1024]{1,0:T(8,128)(2,1)S(1)} %whiten.2.rest_0_, f32[2,16,8,512]{3,2,1,0:T(8,128)S(1)} %shard_map.46.rest_1_), custom_call_target="tpu_custom_call", output_to_operand_aliasing={{}: (2, {})} | custom-call | flops 67108864 | bytes 1048576 | tf_op jit(solution)/shard_map/pallas_call | solution.py:297
  40.4 0.6 %shard_map.48.rest_1_ = f32[2,16,8,512]{3,2,1,0:T(8,128)S(1)} custom-call(f32[8,16,64,128]{3,2,1,0:T(8,128)S(1)} %spectra.1, bf16[64,1024]{1,0:T(8,128)(2,1)S(1)} %collective-permute-done.13.rest_0_, f32[2,16,8,512]{3,2,1,0:T(8,128)S(1)} %shard_map.47.rest_1_), custom_call_target="tpu_custom_call", output_to_operand_aliasing={{}: (2, {})} | custom-call | flops 67108864 | bytes 1048576 | tf_op jit(solution)/shard_map/pallas_call | solution.py:297
  41.0 0.6 %shard_map.49.rest_1_ = f32[2,16,8,512]{3,2,1,0:T(8,128)S(1)} custom-call(f32[8,16,64,128]{3,2,1,0:T(8,128)S(1)} %spectra.1, bf16[64,1024]{1,0:T(8,128)(2,1)S(1)} %collective-permute-done.12.rest_0_, f32[2,16,8,512]{3,2,1,0:T(8,128)S(1)} %shard_map.48.rest_1_), custom_call_target="tpu_custom_call", output_to_operand_aliasing={{}: (2, {})} | custom-call | flops 67108864 | bytes 1048576 | tf_op jit(solution)/shard_map/pallas_call | solution.py:297
  41.6 0.6 %shard_map.50.rest_1_ = f32[2,16,8,512]{3,2,1,0:T(8,128)S(1)} custom-call(f32[8,16,64,128]{3,2,1,0:T(8,128)S(1)} %spectra.1, bf16[64,1024]{1,0:T(8,128)(2,1)S(1)} %collective-permute-done.11.rest_0_, f32[2,16,8,512]{3,2,1,0:T(8,128)S(1)} %shard_map.49.rest_1_), custom_call_target="tpu_custom_call", output_to_operand_aliasing={{}: (2, {})} | custom-call | flops 67108864 | bytes 1048576 | tf_op jit(solution)/shard_map/pallas_call | solution.py:297
  42.3 0.6 %shard_map.51.rest_1_ = f32[2,16,8,512]{3,2,1,0:T(8,128)S(1)} custom-call(f32[8,16,64,128]{3,2,1,0:T(8,128)S(1)} %spectra.1, bf16[64,1024]{1,0:T(8,128)(2,1)S(1)} %collective-permute-done.9.rest_0_, f32[2,16,8,512]{3,2,1,0:T(8,128)S(1)} %shard_map.50.rest_1_), custom_call_target="tpu_custom_call", output_to_operand_aliasing={{}: (2, {})} | custom-call | flops 67108864 | bytes 1048576 | tf_op jit(solution)/shard_map/pallas_call | solution.py:297
  42.9 0.6 %shard_map.52.rest_1_ = f32[2,16,8,512]{3,2,1,0:T(8,128)S(1)} custom-call(f32[8,16,64,128]{3,2,1,0:T(8,128)S(1)} %spectra.1, bf16[64,1024]{1,0:T(8,128)(2,1)S(1)} %collective-permute-done.8.rest_0_, f32[2,16,8,512]{3,2,1,0:T(8,128)S(1)} %shard_map.51.rest_1_), custom_call_target="tpu_custom_call", output_to_operand_aliasing={{}: (2, {})} | custom-call | flops 67108864 | bytes 1048576 | tf_op jit(solution)/shard_map/pallas_call | solution.py:297
  43.6 0.4 shard_map.54
  44.0 0.4 shard_map.53
  44.4 1.0 %collective-permute-done.14 = bf16[16,8,512]{2,1,0:T(8,128)(2,1)S(1)} collective-permute-done((bf16[16,8,512]{2,1,0:T(8,128)(2,1)S(1)}, bf16[16,8,512]{2,1,0:T(8,128)(2,1)S(1)}, u32[]{:S(2)}, u32[]{:S(2)}) %collective-permute-start.14) | collective-permute-done | bytes 131104 | tf_op jit(solution)/shard_map/ppermute | solution.py:363
  45.3 0.7 %add_multiply_fusion = f32[16,8,512]{2,1,0:T(8,128)} fusion(f32[16,8,512]{2,1,0:T(8,128)S(1)} %shard_map.53, bf16[16,8,512]{2,1,0:T(8,128)(2,1)S(1)} %collective-permute-done.14), kind=kLoop, calls=%fused_computation | loop fusion | flops 196608 | bytes 655360 | tf_op jit(solution)/shard_map/div | solution.py:365
  (17 shorter events, 0.3 us)
Async XLA Ops:
  0.0 26.8 %copy-start = (bf16[1024,1024]{1,0:T(8,128)(2,1)S(1)}, bf16[1024,1024]{1,0:T(8,128)(2,1)}, u32[]{:S(2)}) copy-start(bf16[1024,1024]{1,0:T(8,128)(2,1)} %constant.25.clone.table) | copy-start | bytes 6291460
  0.0 6.7 %copy-start.2 = (s32[8]{0:T(128)S(1)}, s32[8]{0:T(128)}, u32[]{:S(2)}) copy-start(s32[8]{0:T(128)} %sources.3) | copy-start | bytes 100
  2.2 6.5 %collective-permute-start.3 = (bf16[4,16,1024]{2,1,0:T(8,128)(2,1)S(1)}, bf16[4,16,1024]{2,1,0:T(8,128)(2,1)S(1)}, u32[]{:S(2)}, u32[]{:S(2)}) collective-permute-start(bf16[4,16,1024]{2,1,0:T(8,128)(2,1)S(1)} %get-tuple-element.34), channel_id=1, source_target_pairs={{0,2},{2,0},{4,6},{6,4},{8,10},{10,8},{12,14},{14,12},{1,3},{3,1},... | collective-permute-start | bytes 393224 | tf_op jit(solution)/shard_map/ppermute | solution.py:322
  5.2 5.2 %collective-permute-start.4 = (bf16[4,16,1024]{2,1,0:T(8,128)(2,1)S(1)}, bf16[4,16,1024]{2,1,0:T(8,128)(2,1)S(1)}, u32[]{:S(2)}, u32[]{:S(2)}) collective-permute-start(bf16[4,16,1024]{2,1,0:T(8,128)(2,1)S(1)} %get-tuple-element.35), channel_id=1, source_target_pairs={{0,4},{2,6},{4,0},{6,2},{8,12},{10,14},{12,8},{14,10},{1,5},{3,7},... | collective-permute-start | bytes 393224 | tf_op jit(solution)/shard_map/ppermute | solution.py:322
  8.2 5.9 %collective-permute-start.5 = (bf16[4,16,1024]{2,1,0:T(8,128)(2,1)S(1)}, bf16[4,16,1024]{2,1,0:T(8,128)(2,1)S(1)}, u32[]{:S(2)}, u32[]{:S(2)}) collective-permute-start(bf16[4,16,1024]{2,1,0:T(8,128)(2,1)S(1)} %get-tuple-element.36), channel_id=1, source_target_pairs={{0,6},{2,4},{4,2},{6,0},{8,14},{10,12},{12,10},{14,8},{1,7},{3,5},... | collective-permute-start | bytes 393224 | tf_op jit(solution)/shard_map/ppermute | solution.py:322
  15.3 11.5 %collective-permute-start.10 = (bf16[8,8,1024]{2,1,0:T(8,128)(2,1)S(1)}, bf16[8,8,1024]{2,1,0:T(8,128)(2,1)S(1)}, u32[]{:S(2)}, u32[]{:S(2)}) collective-permute-start(bf16[8,8,1024]{2,1,0:T(8,128)(2,1)S(1)} %get-tuple-element.45.mine), channel_id=1, source_target_pairs={{0,8},{2,10},{4,12},{6,14},{8,0},{10,2},{12,4},{14,6},{1,9},{3,11}... | collective-permute-start | bytes 393224 | tf_op jit(solution)/shard_map/ppermute | solution.py:322
  18.0 17.2 %copy-start.1 = (s32[16,64]{1,0:T(8,128)S(1)}, s32[16,64]{1,0:T(8,128)}, u32[]{:S(2)}) copy-start(s32[16,64]{1,0:T(8,128)} %valid.3) | copy-start | bytes 12292
  18.0 13.0 %collective-permute-start.6 = (bf16[8,8,1024]{2,1,0:T(8,128)(2,1)S(1)}, bf16[8,8,1024]{2,1,0:T(8,128)(2,1)S(1)}, u32[]{:S(2)}, u32[]{:S(2)}) collective-permute-start(bf16[8,8,1024]{2,1,0:T(8,128)(2,1)S(1)} %get-tuple-element.44.mine), channel_id=1, source_target_pairs={{0,8},{2,10},{4,12},{6,14},{8,0},{10,2},{12,4},{14,6},{1,9},{3,11}... | collective-permute-start | bytes 393224 | tf_op jit(solution)/shard_map/ppermute | solution.py:322
  27.5 7.4 %collective-permute-start.13 = (bf16[64,1024]{1,0:T(8,128)(2,1)S(1)}, bf16[64,1024]{1,0:T(8,128)(2,1)S(1)}, u32[]{:S(2)}, u32[]{:S(2)}) collective-permute-start(bf16[64,1024]{1,0:T(8,128)(2,1)S(1)} %whiten.3.rest_0_), channel_id=1, source_target_pairs={{0,6},{2,4},{4,2},{6,0},{8,14},{10,12},{12,10},{14,8},{1,7},{3,5},... | collective-permute-start | bytes 393224 | tf_op jit(solution)/shard_map/ppermute | solution.py:322
  27.6 13.4 %collective-permute-start.12 = (bf16[64,1024]{1,0:T(8,128)(2,1)S(1)}, bf16[64,1024]{1,0:T(8,128)(2,1)S(1)}, u32[]{:S(2)}, u32[]{:S(2)}) collective-permute-start(bf16[64,1024]{1,0:T(8,128)(2,1)S(1)} %whiten.3.rest_0_), channel_id=1, source_target_pairs={{0,2},{2,0},{4,6},{6,4},{8,10},{10,8},{12,14},{14,12},{1,3},{3,1},... | collective-permute-start | bytes 393224 | tf_op jit(solution)/shard_map/ppermute | solution.py:322
  28.4 13.2 %collective-permute-start.11 = (bf16[64,1024]{1,0:T(8,128)(2,1)S(1)}, bf16[64,1024]{1,0:T(8,128)(2,1)S(1)}, u32[]{:S(2)}, u32[]{:S(2)}) collective-permute-start(bf16[64,1024]{1,0:T(8,128)(2,1)S(1)} %whiten.3.rest_0_), channel_id=1, source_target_pairs={{0,4},{2,6},{4,0},{6,2},{8,12},{10,14},{12,8},{14,10},{1,5},{3,7},... | collective-permute-start | bytes 393224 | tf_op jit(solution)/shard_map/ppermute | solution.py:322
  31.7 10.6 %collective-permute-start.9 = (bf16[64,1024]{1,0:T(8,128)(2,1)S(1)}, bf16[64,1024]{1,0:T(8,128)(2,1)S(1)}, u32[]{:S(2)}, u32[]{:S(2)}) collective-permute-start(bf16[64,1024]{1,0:T(8,128)(2,1)S(1)} %whiten.2.rest_0_), channel_id=1, source_target_pairs={{0,6},{2,4},{4,2},{6,0},{8,14},{10,12},{12,10},{14,8},{1,7},{3,5},... | collective-permute-start | bytes 393224 | tf_op jit(solution)/shard_map/ppermute | solution.py:322
  32.0 10.9 %collective-permute-start.8 = (bf16[64,1024]{1,0:T(8,128)(2,1)S(1)}, bf16[64,1024]{1,0:T(8,128)(2,1)S(1)}, u32[]{:S(2)}, u32[]{:S(2)}) collective-permute-start(bf16[64,1024]{1,0:T(8,128)(2,1)S(1)} %whiten.2.rest_0_), channel_id=1, source_target_pairs={{0,2},{2,0},{4,6},{6,4},{8,10},{10,8},{12,14},{14,12},{1,3},{3,1},... | collective-permute-start | bytes 393224 | tf_op jit(solution)/shard_map/ppermute | solution.py:322
  34.9 8.6 %collective-permute-start.7 = (bf16[64,1024]{1,0:T(8,128)(2,1)S(1)}, bf16[64,1024]{1,0:T(8,128)(2,1)S(1)}, u32[]{:S(2)}, u32[]{:S(2)}) collective-permute-start(bf16[64,1024]{1,0:T(8,128)(2,1)S(1)} %whiten.2.rest_0_), channel_id=1, source_target_pairs={{0,4},{2,6},{4,0},{6,2},{8,12},{10,14},{12,8},{14,10},{1,5},{3,7},... | collective-permute-start | bytes 393224 | tf_op jit(solution)/shard_map/ppermute | solution.py:322
  43.9 1.4 %collective-permute-start.14 = (bf16[16,8,512]{2,1,0:T(8,128)(2,1)S(1)}, bf16[16,8,512]{2,1,0:T(8,128)(2,1)S(1)}, u32[]{:S(2)}, u32[]{:S(2)}) collective-permute-start(bf16[16,8,512]{2,1,0:T(8,128)(2,1)S(1)} %shard_map.54), channel_id=1, source_target_pairs={{0,1},{1,0},{2,3},{3,2},{4,5},{5,4},{6,7},{7,6},{8,9},{9,8},{10,11... | collective-permute-start | bytes 393224 | tf_op jit(solution)/shard_map/ppermute | solution.py:363
where the time goes:
time: 46.3 us; the launch traced here: 46.1 us
  waiting for transfers between devices  17.1 us (37%)
  Pallas kernels  13.5 us (29%)
  starting transfers between devices  13.1 us (28%)
  other arithmetic  1.56 us (3%)
  between operations  0.84 us (2%)
    ppermute x11, waiting for transfers between devices, swap(): return lax.ppermute(value, 'chan', [(i, i ^ bit) for i in range(n_chan)])  16.1 us
    ppermute x11, starting transfers between devices, swap(): return lax.ppermute(value, 'chan', [(i, i ^ bit) for i in range(n_chan)])  13 us
    pallas_call x9, Pallas kernels, cross_of(): pl.pallas_call(functools.partial(cross_kernel, places, mode, acc is None)...  5.01 us
    pallas_call x1, Pallas kernels, spectra_of(): pl.pallas_call(functools.partial(spectra_kernel, chans), out_shape=jax.Sh...  3.92 us
    pallas_call x1, Pallas kernels, pick(): pl.pallas_call(pick_kernel, out_shape=(parts[0],) * QUAD + (parts[1],) *...  2.18 us
    pallas_call x2, Pallas kernels, whitened_of(): pl.pallas_call(whiten_kernel, out_shape=jax.ShapeDtypeStruct((rows, width...  1.26 us
    pallas_call x1, Pallas kernels, merge(): pl.pallas_call(functools.partial(merge_kernel, per_dev), out_shape=(part,...  1.12 us
    ppermute x1, waiting for transfers between devices, stacks(): came = lax.ppermute(send, 'rec', [(i, i ^ 1) for i in range(n_rec)])  0.97 us
  transfers between devices with their start and end apart: 12, of which 6 were waited for; matrix products, arithmetic and copies ran while one was open for 2% of the time, Pallas kernels for 21%

commit v1 on v0

--- a/solution.py
+++ b/solution.py
@@ -35,11 +35,60 @@
 
 
 def owner_of(sources, per_dev, s):
-    owner = sources[s] // per_dev
+    owner = lax.div(sources[s], per_dev)
     rank = jnp.int32(0)
     for before in range(s):
-        rank += (sources[before] // per_dev == owner).astype(jnp.int32)
+        rank += (lax.div(sources[before], per_dev) == owner).astype(jnp.int32)
     return owner, rank
+
+
+def plan_kernel(per_dev, room, packed, sources, plan):
+    n_src = sources.shape[0]
+    rounds = 2 * QUAD * room
+    me = lax.axis_index("chan")
+    for i in range(rounds):
+        plan[i] = jnp.int32(-1)
+    owners = [lax.div(sources[s], per_dev) for s in range(n_src)]
+    quads = [lax.div(owner, QUAD) for owner in owners]
+    crowded = jnp.int32(0)
+    counts = [jnp.int32(0), jnp.int32(0)]
+    for s in range(n_src):
+        rank = jnp.int32(0)
+        for before in range(s):
+            rank += (owners[before] == owners[s]).astype(jnp.int32)
+        crowded = jnp.maximum(crowded, rank + 1)
+        place = jnp.int32(s)
+        if packed:
+            place = jnp.where(quads[s] == 0, counts[0], n_src - 1 - counts[1])
+            counts[0] += (quads[s] == 0).astype(jnp.int32)
+            counts[1] += (quads[s] != 0).astype(jnp.int32)
+        plan[rounds + place] = jnp.int32(s)
+        later = (rank >= room).astype(jnp.int32)
+        member = lax.rem(owners[s], QUAD) ^ lax.rem(me, QUAD)
+
+        @pl.when(quads[s] == lax.div(me, QUAD))
+        def _():
+            plan[(later * QUAD + member) * room + rank - later * room] = place
+
+    plan[rounds + n_src] = (crowded > room).astype(jnp.int32)
+    most = jnp.maximum(counts[0], counts[1])
+    plan[rounds + n_src + 1] = (most > n_src - spare_of(n_src)).astype(jnp.int32)
+
+
+def spare_of(n_src):
+    return n_src // 4
+
+
+def plan_of(sources, per_dev, room, packed):
+    size = 2 * QUAD * room + sources.shape[0] + 2
+    return pl.pallas_call(
+        functools.partial(plan_kernel, per_dev, room, packed),
+        out_shape=jax.ShapeDtypeStruct((size,), jnp.int32),
+        in_specs=[SMEM],
+        out_specs=SMEM,
+        compiler_params=ROOM,
+        name="plan",
+    )(sources)
 
 
 def pick_kernel(sources, valid, records, *rest):
@@ -112,48 +161,64 @@
     )(*args)
 
 
-def merge_kernel(per_dev, sources, *refs):
-    firsts, others, outs = refs[:QUAD], refs[QUAD : 2 * QUAD], refs[2 * QUAD :]
-    room = firsts[0].shape[0]
-    part = outs[0].shape[1]
-    me = lax.axis_index("chan")
-    for s in range(sources.shape[0]):
-        owner, rank = owner_of(sources, per_dev, s)
-        near = owner // QUAD == me // QUAD
-
-        def put(rows):
-            for t, out in enumerate(outs):
-                out[s] = rows[t * part : (t + 1) * part]
-
-        @pl.when(jnp.logical_not(near))
-        def _():
-            for out in outs:
-                out[s] = jnp.zeros(out.shape[1:], out.dtype)
-
+def merge_kernel(spare, plan, *refs):
+    parts, outs = refs[: 2 * QUAD], refs[2 * QUAD :]
+    room = parts[0].shape[0]
+    n_src, rows = outs[0].shape[:2]
+    upper = lax.rem(lax.div(lax.axis_index("chan"), QUAD), 2) == 1
+    for out in outs:
+        out[...] = jnp.zeros(out.shape, out.dtype)
+
+    def put(block, place):
+        for t in range(STREAMS):
+            half = block[t * rows : (t + 1) * rows]
+            outs[t][place] = half
+            if not spare:
+                continue
+            sent, left = outs[STREAMS + t], outs[2 * STREAMS + t]
+            depth = jnp.where(upper, place - spare, place)
+            fits = jnp.logical_and(depth >= 0, depth < n_src - spare)
+
+            @pl.when(fits)
+            def _():
+                sent[jnp.clip(depth, 0, n_src - spare - 1)] = half
+
+            @pl.when(jnp.logical_not(fits))
+            def _():
+                left[jnp.where(upper, place, place - n_src + spare)] = half
+
+    def put_round(later):
         for j in range(QUAD):
-            here = jnp.logical_and(near, lax.rem(owner, QUAD) ^ lax.rem(me, QUAD) == j)
-
-            @pl.when(jnp.logical_and(here, rank < room))
-            def _():
-                put(firsts[j][jnp.minimum(rank, room - 1)])
-
-            @pl.when(jnp.logical_and(here, rank >= room))
-            def _():
-                put(others[j][jnp.maximum(rank - room, 0)])
-
-
-def merge(sources, per_dev, firsts, others):
-    n_src = sources.shape[0]
-    _, block, length = firsts[0].shape
-    part = jax.ShapeDtypeStruct((n_src, block // STREAMS, length), firsts[0].dtype)
-    return pl.pallas_call(
-        functools.partial(merge_kernel, per_dev),
-        out_shape=(part,) * STREAMS,
+            for k in range(room):
+                place = plan[(later * QUAD + j) * room + k]
+
+                @pl.when(place >= 0)
+                def _():
+                    put(parts[later * QUAD + j][k], place)
+
+    put_round(0)
+
+    @pl.when(plan[2 * QUAD * room + n_src] == 1)
+    def _():
+        put_round(1)
+
+
+def merge(plan, n_src, spare, parts):
+    _, block, length = parts[0].shape
+    dtype = parts[0].dtype
+    sizes = [n_src, n_src - spare, spare] if spare else [n_src]
+    return pl.pallas_call(
+        functools.partial(merge_kernel, spare),
+        out_shape=[
+            jax.ShapeDtypeStruct((size, block // STREAMS, length), dtype)
+            for size in sizes
+            for _ in range(STREAMS)
+        ],
         in_specs=[SMEM] + [VMEM] * (2 * QUAD),
-        out_specs=(VMEM,) * STREAMS,
+        out_specs=[VMEM] * (len(sizes) * STREAMS),
         compiler_params=ROOM,
         name="merge",
-    )(sources, *firsts, *others)
+    )(plan, *parts)
 
 
 def spectra_kernel(chans, valid, table, records, out, buf, sems):
@@ -202,11 +267,35 @@
     )(valid, table, records)
 
 
-def whiten_kernel(table, mine, other, out, mixed):
+def whiten_kernel(spare, plan, table, mine, *rest):
+    (*came, out, mixed, rows) = rest
     n_src, block, length = mine.shape
     bins = table.shape[1] // 2
-    rows = (mine[...] + other[...]).reshape(n_src * block, length)
-    spec = jnp.dot(rows, table[...], preferred_element_type=jnp.float32)
+    base = plan.shape[0] - 2 - n_src
+    upper = lax.rem(lax.div(lax.axis_index("chan"), QUAD), 2) == 1
+
+    def arrived(place, high):
+        if not spare:
+            return came[0][place]
+        if high:
+            first, second = place, place - n_src + spare
+        else:
+            first, second = place - spare, place
+        fits = 0 <= first < n_src - spare
+        return came[0][first] if fits else came[1][second]
+
+    for high in (False, True):
+
+        @pl.when(upper == high)
+        def _():
+            for place in range(n_src):
+                rows[plan[base + place]] = mine[place] + arrived(place, high)
+
+    spec = jnp.dot(
+        rows[...].reshape(n_src * block, length),
+        table[...],
+        preferred_element_type=jnp.float32,
+    )
     real, imag = spec[:, :bins], spec[:, bins:]
     power = jnp.sum(real * real + imag * imag, axis=1, keepdims=True) / bins
     white = spec * lax.rsqrt(power + 1e-06)
@@ -217,19 +306,22 @@
         out[:, f : f + LANES] = mixed[f // LANES].astype(out.dtype)
 
 
-def whitened_of(table, mine, other):
-    n_src, block, _ = mine.shape
+def whitened_of(plan, table, spare, mine, came):
+    n_src, block, length = mine.shape
     width = table.shape[1]
     rows = n_src * block
     return pl.pallas_call(
-        whiten_kernel,
+        functools.partial(whiten_kernel, spare),
         out_shape=jax.ShapeDtypeStruct((rows, width), jnp.bfloat16),
-        in_specs=[VMEM, VMEM, VMEM],
+        in_specs=[SMEM] + [VMEM] * (2 + len(came)),
         out_specs=VMEM,
-        scratch_shapes=[pltpu.VMEM((width // LANES, rows, LANES), jnp.float32)],
+        scratch_shapes=[
+            pltpu.VMEM((width // LANES, rows, LANES), jnp.float32),
+            pltpu.VMEM((n_src, block, length), mine.dtype),
+        ],
         compiler_params=ROOM,
         name="whiten",
-    )(table, mine, other)
+    )(plan, table, mine, *came)
 
 
 def cross_kernel(places, mode, first, spectra, *rest):
@@ -325,29 +417,47 @@
     picked = pick(sources, valid, records, room)
     first, more = picked[:QUAD], picked[QUAD:]
     came = {j: swap(first[j], j) for j in (3, 1, 2)}
-    owners = sources // per_dev
-    held = jnp.sum(owners[:, None] == owners[None, :], axis=1)
-
-    def scatter_more(parts):
-        return [lax.ppermute(x, "chan", [(i, i ^ (j + 1)) for i in range(n_chan)]) for j, x in enumerate(parts)]
-
-    rest = lax.cond(jnp.max(held) > room, scatter_more, lambda parts: parts, list(more[1:]))
-    parts = merge(sources, per_dev, [first[0], came[1], came[2], came[3]], [more[0], *rest])
+    packed = n_chan == 2 * QUAD
+    spare = spare_of(n_src) if packed else 0
+    plan = plan_of(sources, per_dev, room, packed)
+
+    def exchange(bits):
+        def run(parts):
+            return [
+                lax.ppermute(x, "chan", [(i, i ^ bit) for i in range(n_chan)])
+                for x, bit in zip(parts, bits)
+            ]
+
+        return run
+
+    def same(parts):
+        return parts
+
+    rest = lax.cond(plan[-2] > 0, exchange((1, 2, 3)), same, list(more[1:]))
+    parts = merge(plan, n_src, spare, [first[0], came[1], came[2], came[3], more[0], *rest])
+    homes, sent, left = parts[:STREAMS], parts[STREAMS : 2 * STREAMS], parts[2 * STREAMS :]
     last = n_chan // 2
-    homes = []
-    for t in range(STREAMS):
-        home = parts[t]
-        bit = QUAD
-        while bit < last:
-            home = home + swap(home, bit)
-            bit *= 2
-        homes.append((home, swap(home, last)))
+    others = []
+    if packed:
+        for t in range(STREAMS):
+            others.append([swap(sent[t], last)])
+        left = lax.cond(plan[-1] > 0, exchange((last,) * STREAMS), same, list(left))
+        *left, valid = lax.optimization_barrier((*left, valid))
+        for t in range(STREAMS):
+            others[t].append(left[t])
+    else:
+        homes = list(homes)
+        for t in range(STREAMS):
+            bit = QUAD
+            while bit < last:
+                homes[t] = homes[t] + swap(homes[t], bit)
+                bit *= 2
+            others.append([swap(homes[t], last)])
     spectra = spectra_of(valid, table, records)
     acc = None
     gathered = []
     for t in range(STREAMS):
-        home, other = homes[t]
-        white = whitened_of(table, home, other)
+        white = whitened_of(plan, table, spare, homes[t], others[t])
         blocks = [((0, t), white)]
         for j in (3, 1, 2):
             blocks.append(((j, t), swap(white, j)))

time: 46.3 us -> 45.5 us (0.983)
  waiting for transfers between devices: 17.1 us -> 10.3 us
  starting transfers between devices: 13.1 us -> 16.7 us
  Pallas kernels: 13.5 us -> 15.5 us
  other arithmetic: 1.56 us -> 0.74 us
  local copies, waits for them, and re-layouts: 0.01 us -> 0.6 us
  between operations: 0.84 us -> 1.43 us
    ppermute x11, waiting for transfers between devices: 16.1 us -> 9.36 us  [swap(): return lax.ppermute(value, 'chan', [(i, i ^ bit) for i in range(n_chan)])]
    ppermute x11, starting transfers between devices: 13 us -> 16.6 us  [swap(): return lax.ppermute(value, 'chan', [(i, i ^ bit) for i in range(n_chan)])]
    pallas_call x3 -> x4, Pallas kernels: 2.39 us -> 4.46 us  [the longest x2 2.41 us: whitened_of(): pl.pallas_call(functools.partial(whiten_kernel, spare), out_shape=jax.Sha...]
    reduce_max x1 -> x0, other arithmetic: 0.64 us -> none  [stacks(): jnp.max(held) > room]
    slice x0 -> x1, local copies, waits for them, and re-layouts: none -> 0.59 us  [stacks(): rest = lax.cond(plan[-2] > 0, exchange((1, 2, 3)), same, list(more[1:]))]
  transfers between devices with their start and end apart: 12 -> 12, of which waited for: 6 -> 5; matrix products, arithmetic and copies ran while one was open for 2% -> 1% of each run, Pallas kernels for 21% -> 24%
where the time goes in v1:
time: 45.5 us; the launch traced here: 45.3 us
  starting transfers between devices  16.7 us (37%)
  Pallas kernels  15.5 us (34%)
  waiting for transfers between devices  10.3 us (23%)
  between operations  1.43 us (3%)
  other arithmetic  0.74 us (2%)
  local copies, waits for them, and re-layouts  0.6 us (1%)
    ppermute x11, starting transfers between devices, swap(): return lax.ppermute(value, 'chan', [(i, i ^ bit) for i in range(n_chan)])  16.6 us
    ppermute x11, waiting for transfers between devices, swap(): return lax.ppermute(value, 'chan', [(i, i ^ bit) for i in range(n_chan)])  9.36 us
    pallas_call x9, Pallas kernels, cross_of(): pl.pallas_call(functools.partial(cross_kernel, places, mode, acc is None)...  5.01 us
    pallas_call x1, Pallas kernels, spectra_of(): pl.pallas_call(functools.partial(spectra_kernel, chans), out_shape=jax.Sh...  3.93 us
    pallas_call x2, Pallas kernels, whitened_of(): pl.pallas_call(functools.partial(whiten_kernel, spare), out_shape=jax.Sha...  2.41 us
    pallas_call x1, Pallas kernels, pick(): pl.pallas_call(pick_kernel, out_shape=(parts[0],) * QUAD + (parts[1],) *...  2.08 us
    pallas_call x1, Pallas kernels, plan_of(): pl.pallas_call(functools.partial(plan_kernel, per_dev, room, packed), out...  1.27 us
    ppermute x1, waiting for transfers between devices, stacks(): came = lax.ppermute(send, 'rec', [(i, i ^ 1) for i in range(n_rec)])  0.97 us
  transfers between devices with their start and end apart: 12, of which 5 were waited for; matrix products, arithmetic and copies ran while one was open for 1% of the time, Pallas kernels for 24%

profile of v1, /device:TPU:0, one launch (start us, length us, event | category | flops | bytes accessed | tf_op | source)
XLA Modules:
  0.0 45.3 jit_solution(13506201178427255501)
XLA Ops:
  0.0 2.1 %pick.1 = (bf16[4,16,1024]{2,1,0:T(8,128)(2,1)S(1)}, bf16[4,16,1024]{2,1,0:T(8,128)(2,1)S(1)}, bf16[4,16,1024]{2,1,0:T(8,128)(2,1)S(1)}, bf16[4,16,1024]{2,1,0:T...) custom-call(s32[8]{0:T(128)} %sources.3, ...), custom_call_target="tpu_custom_call" | custom-call | tf_op jit(solution)/shard_map/pick/pallas_call | solution.py:148
  2.1 3.0 %collective-permute-start.5 = (bf16[4,16,1024]{2,1,0:T(8,128)(2,1)S(1)}, bf16[4,16,1024]{2,1,0:T(8,128)(2,1)S(1)}, u32[]{:S(2)}, u32[]{:S(2)}) collective-permute-start(bf16[4,16,1024]{2,1,0:T(8,128)(2,1)S(1)} %get-tuple-element.53), channel_id=1, source_target_pairs={{0,2},{2,0},{4,6},{6,4},{8,10},{10,8},{12,14},{14,12},{1,3},{3,1},... | collective-permute-start | bytes 393224 | tf_op jit(solution)/shard_map/ppermute | solution.py:414
  5.1 1.5 %collective-permute-start.6 = (bf16[4,16,1024]{2,1,0:T(8,128)(2,1)S(1)}, bf16[4,16,1024]{2,1,0:T(8,128)(2,1)S(1)}, u32[]{:S(2)}, u32[]{:S(2)}) collective-permute-start(bf16[4,16,1024]{2,1,0:T(8,128)(2,1)S(1)} %get-tuple-element.54), channel_id=1, source_target_pairs={{0,4},{2,6},{4,0},{6,2},{8,12},{10,14},{12,8},{14,10},{1,5},{3,7},... | collective-permute-start | bytes 393224 | tf_op jit(solution)/shard_map/ppermute | solution.py:414
  6.6 1.3 %plan.1 = s32[42]{0:T(128)S(1)} custom-call(s32[8]{0:T(128)S(1)} %copy-done.2), custom_call_target="tpu_custom_call" | custom-call | tf_op jit(solution)/shard_map/plan/pallas_call | solution.py:84
  7.9 0.6 %fusion = (s32[1]{0:T(128)}, s32[1]{0:T(128)}) fusion(s32[42]{0:T(128)S(1)} %plan.1), kind=kLoop, calls=%fused_computation.1 | loop fusion | bytes 16 | tf_op jit(solution)/shard_map/slice | solution.py:436
  9.2 0.2 collective-permute-start.7
  9.4 0.7 %collective-permute-done.6.refs_2_ = bf16[4,16,1024]{2,1,0:T(8,128)(2,1)S(1)} collective-permute-done((bf16[4,16,1024]{2,1,0:T(8,128)(2,1)S(1)}, bf16[4,16,1024]{2,1,0:T(8,128)(2,1)S(1)}, u32[]{:S(2)}, u32[]{:S(2)}) %collective-permute-start.6) | collective-permute-done | bytes 131104 | tf_op jit(solution)/shard_map/ppermute | solution.py:414
  10.1 5.0 %collective-permute-done.7.refs_3_ = bf16[4,16,1024]{2,1,0:T(8,128)(2,1)S(1)} collective-permute-done((bf16[4,16,1024]{2,1,0:T(8,128)(2,1)S(1)}, bf16[4,16,1024]{2,1,0:T(8,128)(2,1)S(1)}, u32[]{:S(2)}, u32[]{:S(2)}) %collective-permute-start.7) | collective-permute-done | bytes 131104 | tf_op jit(solution)/shard_map/ppermute | solution.py:414
  15.1 0.8 %merge.1 = (bf16[8,8,1024]{2,1,0:T(8,128)(2,1)S(1)}, bf16[8,8,1024]{2,1,0:T(8,128)(2,1)S(1)}, bf16[6,8,1024]{2,1,0:T(8,128)(2,1)S(1)}, bf16[6,8,1024]{2,1,0:T(8,...) custom-call(s32[42]{0:T(128)S(1)} %plan.1, ...), custom_call_target="tpu_custom_call" | custom-call | tf_op jit(solution)/shard_map/merge/pallas_call | solution.py:210
  15.9 2.8 %collective-permute-start.12 = (bf16[6,8,1024]{2,1,0:T(8,128)(2,1)S(1)}, bf16[6,8,1024]{2,1,0:T(8,128)(2,1)S(1)}, u32[]{:S(2)}, u32[]{:S(2)}) collective-permute-start(bf16[6,8,1024]{2,1,0:T(8,128)(2,1)S(1)} %get-tuple-element.72), channel_id=1, source_target_pairs={{0,8},{2,10},{4,12},{6,14},{8,0},{10,2},{12,4},{14,6},{1,9},{3,11}... | collective-permute-start | bytes 294920 | tf_op jit(solution)/shard_map/ppermute | solution.py:414
  19.3 3.2 %collective-permute-done.12.rest_0_ = bf16[6,8,1024]{2,1,0:T(8,128)(2,1)S(1)} collective-permute-done((bf16[6,8,1024]{2,1,0:T(8,128)(2,1)S(1)}, bf16[6,8,1024]{2,1,0:T(8,128)(2,1)S(1)}, u32[]{:S(2)}, u32[]{:S(2)}) %collective-permute-start.12) | collective-permute-done | bytes 98336 | tf_op jit(solution)/shard_map/ppermute | solution.py:414
  22.5 1.2 %whiten.3.rest_0_ = bf16[64,1024]{1,0:T(8,128)(2,1)S(1)} custom-call(s32[42]{0:T(128)S(1)} %plan.1, bf16[1024,1024]{1,0:T(8,128)(2,1)S(1)} %copy-done, bf16[8,8,1024]{2,1,0:T(8,128)(2,1)S(1)} %get-tuple-element.71.mine, bf16[6,8,1024]{2,1,0:T(8,128)(2,1)S(1)} %collective-permute-done.12.rest_0_, bf16[2,8,1024]{2,1,0:T(8,128)(2,1)S(1)} %get-tuple-element.73.rest_1_), custom_call_target="tpu_custom_call" | custom-call | tf_op jit(solution)/shard_map/whiten/pallas_call | solution.py:313
  23.7 0.1 collective-permute-start.15
  23.8 1.9 %collective-permute-start.8 = (bf16[6,8,1024]{2,1,0:T(8,128)(2,1)S(1)}, bf16[6,8,1024]{2,1,0:T(8,128)(2,1)S(1)}, u32[]{:S(2)}, u32[]{:S(2)}) collective-permute-start(bf16[6,8,1024]{2,1,0:T(8,128)(2,1)S(1)} %get-tuple-element.69), channel_id=1, source_target_pairs={{0,8},{2,10},{4,12},{6,14},{8,0},{10,2},{12,4},{14,6},{1,9},{3,11}... | collective-permute-start | bytes 294920 | tf_op jit(solution)/shard_map/ppermute | solution.py:414
  25.7 1.7 %collective-permute-start.14 = (bf16[64,1024]{1,0:T(8,128)(2,1)S(1)}, bf16[64,1024]{1,0:T(8,128)(2,1)S(1)}, u32[]{:S(2)}, u32[]{:S(2)}) collective-permute-start(bf16[64,1024]{1,0:T(8,128)(2,1)S(1)} %whiten.3.rest_0_), channel_id=1, source_target_pairs={{0,2},{2,0},{4,6},{6,4},{8,10},{10,8},{12,14},{14,12},{1,3},{3,1},... | collective-permute-start | bytes 393224 | tf_op jit(solution)/shard_map/ppermute | solution.py:414
  27.4 1.6 %collective-permute-start.13 = (bf16[64,1024]{1,0:T(8,128)(2,1)S(1)}, bf16[64,1024]{1,0:T(8,128)(2,1)S(1)}, u32[]{:S(2)}, u32[]{:S(2)}) collective-permute-start(bf16[64,1024]{1,0:T(8,128)(2,1)S(1)} %whiten.3.rest_0_), channel_id=1, source_target_pairs={{0,4},{2,6},{4,0},{6,2},{8,12},{10,14},{12,8},{14,10},{1,5},{3,7},... | collective-permute-start | bytes 393224 | tf_op jit(solution)/shard_map/ppermute | solution.py:414
  29.0 0.4 collective-permute-done.8.rest_0_
  29.4 1.2 %whiten.2.rest_0_ = bf16[64,1024]{1,0:T(8,128)(2,1)S(1)} custom-call(s32[42]{0:T(128)S(1)} %plan.1, bf16[1024,1024]{1,0:T(8,128)(2,1)S(1)} %copy-done, bf16[8,8,1024]{2,1,0:T(8,128)(2,1)S(1)} %get-tuple-element.68.mine, bf16[6,8,1024]{2,1,0:T(8,128)(2,1)S(1)} %collective-permute-done.8.rest_0_, bf16[2,8,1024]{2,1,0:T(8,128)(2,1)S(1)} %get-tuple-element.70.rest_1_), custom_call_target="tpu_custom_call" | custom-call | tf_op jit(solution)/shard_map/whiten/pallas_call | solution.py:313
  30.7 3.1 %collective-permute-start.11 = (bf16[64,1024]{1,0:T(8,128)(2,1)S(1)}, bf16[64,1024]{1,0:T(8,128)(2,1)S(1)}, u32[]{:S(2)}, u32[]{:S(2)}) collective-permute-start(bf16[64,1024]{1,0:T(8,128)(2,1)S(1)} %whiten.2.rest_0_), channel_id=1, source_target_pairs={{0,6},{2,4},{4,2},{6,0},{8,14},{10,12},{12,10},{14,8},{1,7},{3,5},... | collective-permute-start | bytes 393224 | tf_op jit(solution)/shard_map/ppermute | solution.py:414
  33.7 0.7 %collective-permute-start.10 = (bf16[64,1024]{1,0:T(8,128)(2,1)S(1)}, bf16[64,1024]{1,0:T(8,128)(2,1)S(1)}, u32[]{:S(2)}, u32[]{:S(2)}) collective-permute-start(bf16[64,1024]{1,0:T(8,128)(2,1)S(1)} %whiten.2.rest_0_), channel_id=1, source_target_pairs={{0,2},{2,0},{4,6},{6,4},{8,10},{10,8},{12,14},{14,12},{1,3},{3,1},... | collective-permute-start | bytes 393224 | tf_op jit(solution)/shard_map/ppermute | solution.py:414
  34.4 3.9 %spectra.1 = f32[8,16,64,128]{3,2,1,0:T(8,128)S(1)} custom-call(s32[16,64]{1,0:T(8,128)S(1)} %copy-done.1, bf16[1024,1024]{1,0:T(8,128)(2,1)S(1)} %copy-done, bf16[16,64,1024]{2,1,0:T(8,128)(2,1)} %records.3), custom_call_target="tpu_custom_call" | custom-call | flops 2147483648 | bytes 6291456 | tf_op jit(solution)/shard_map/spectra/pallas_call | solution.py:251
  38.4 0.6 %shard_map.46.rest_1_ = f32[2,16,8,512]{3,2,1,0:T(8,128)S(1)} custom-call(f32[8,16,64,128]{3,2,1,0:T(8,128)S(1)} %spectra.1, bf16[64,1024]{1,0:T(8,128)(2,1)S(1)} %whiten.3.rest_0_), custom_call_target="tpu_custom_call" | custom-call | flops 67108864 | bytes 1048576 | tf_op jit(solution)/shard_map/pallas_call | solution.py:389
  39.0 0.6 %shard_map.47.rest_1_ = f32[2,16,8,512]{3,2,1,0:T(8,128)S(1)} custom-call(f32[8,16,64,128]{3,2,1,0:T(8,128)S(1)} %spectra.1, bf16[64,1024]{1,0:T(8,128)(2,1)S(1)} %whiten.2.rest_0_, f32[2,16,8,512]{3,2,1,0:T(8,128)S(1)} %shard_map.46.rest_1_), custom_call_target="tpu_custom_call", output_to_operand_aliasing={{}: (2, {})} | custom-call | flops 67108864 | bytes 1048576 | tf_op jit(solution)/shard_map/pallas_call | solution.py:389
  39.6 0.6 %shard_map.48.rest_1_ = f32[2,16,8,512]{3,2,1,0:T(8,128)S(1)} custom-call(f32[8,16,64,128]{3,2,1,0:T(8,128)S(1)} %spectra.1, bf16[64,1024]{1,0:T(8,128)(2,1)S(1)} %collective-permute-done.15.rest_0_, f32[2,16,8,512]{3,2,1,0:T(8,128)S(1)} %shard_map.47.rest_1_), custom_call_target="tpu_custom_call", output_to_operand_aliasing={{}: (2, {})} | custom-call | flops 67108864 | bytes 1048576 | tf_op jit(solution)/shard_map/pallas_call | solution.py:389
  40.2 0.6 %shard_map.49.rest_1_ = f32[2,16,8,512]{3,2,1,0:T(8,128)S(1)} custom-call(f32[8,16,64,128]{3,2,1,0:T(8,128)S(1)} %spectra.1, bf16[64,1024]{1,0:T(8,128)(2,1)S(1)} %collective-permute-done.14.rest_0_, f32[2,16,8,512]{3,2,1,0:T(8,128)S(1)} %shard_map.48.rest_1_), custom_call_target="tpu_custom_call", output_to_operand_aliasing={{}: (2, {})} | custom-call | flops 67108864 | bytes 1048576 | tf_op jit(solution)/shard_map/pallas_call | solution.py:389
  40.9 0.6 %shard_map.50.rest_1_ = f32[2,16,8,512]{3,2,1,0:T(8,128)S(1)} custom-call(f32[8,16,64,128]{3,2,1,0:T(8,128)S(1)} %spectra.1, bf16[64,1024]{1,0:T(8,128)(2,1)S(1)} %collective-permute-done.13.rest_0_, f32[2,16,8,512]{3,2,1,0:T(8,128)S(1)} %shard_map.49.rest_1_), custom_call_target="tpu_custom_call", output_to_operand_aliasing={{}: (2, {})} | custom-call | flops 67108864 | bytes 1048576 | tf_op jit(solution)/shard_map/pallas_call | solution.py:389
  41.5 0.6 %shard_map.51.rest_1_ = f32[2,16,8,512]{3,2,1,0:T(8,128)S(1)} custom-call(f32[8,16,64,128]{3,2,1,0:T(8,128)S(1)} %spectra.1, bf16[64,1024]{1,0:T(8,128)(2,1)S(1)} %collective-permute-done.11.rest_0_, f32[2,16,8,512]{3,2,1,0:T(8,128)S(1)} %shard_map.50.rest_1_), custom_call_target="tpu_custom_call", output_to_operand_aliasing={{}: (2, {})} | custom-call | flops 67108864 | bytes 1048576 | tf_op jit(solution)/shard_map/pallas_call | solution.py:389
  42.1 0.6 %shard_map.52.rest_1_ = f32[2,16,8,512]{3,2,1,0:T(8,128)S(1)} custom-call(f32[8,16,64,128]{3,2,1,0:T(8,128)S(1)} %spectra.1, bf16[64,1024]{1,0:T(8,128)(2,1)S(1)} %collective-permute-done.10.rest_0_, f32[2,16,8,512]{3,2,1,0:T(8,128)S(1)} %shard_map.51.rest_1_), custom_call_target="tpu_custom_call", output_to_operand_aliasing={{}: (2, {})} | custom-call | flops 67108864 | bytes 1048576 | tf_op jit(solution)/shard_map/pallas_call | solution.py:389
  42.8 0.4 shard_map.54
  43.2 0.4 shard_map.53
  43.6 1.0 %collective-permute-done.16 = bf16[16,8,512]{2,1,0:T(8,128)(2,1)S(1)} collective-permute-done((bf16[16,8,512]{2,1,0:T(8,128)(2,1)S(1)}, bf16[16,8,512]{2,1,0:T(8,128)(2,1)S(1)}, u32[]{:S(2)}, u32[]{:S(2)}) %collective-permute-start.16) | collective-permute-done | bytes 131104 | tf_op jit(solution)/shard_map/ppermute | solution.py:473
  44.5 0.7 %add_multiply_fusion = f32[16,8,512]{2,1,0:T(8,128)} fusion(f32[16,8,512]{2,1,0:T(8,128)S(1)} %shard_map.53, bf16[16,8,512]{2,1,0:T(8,128)(2,1)S(1)} %collective-permute-done.16), kind=kLoop, calls=%fused_computation | loop fusion | flops 196608 | bytes 655360 | tf_op jit(solution)/shard_map/div | solution.py:475
  (17 shorter events, 0.1 us)
Async XLA Ops:
  0.0 22.5 %copy-start = (bf16[1024,1024]{1,0:T(8,128)(2,1)S(1)}, bf16[1024,1024]{1,0:T(8,128)(2,1)}, u32[]{:S(2)}) copy-start(bf16[1024,1024]{1,0:T(8,128)(2,1)} %constant.9.clone.table) | copy-start | bytes 6291460
  0.0 6.6 %copy-start.2 = (s32[8]{0:T(128)S(1)}, s32[8]{0:T(128)}, u32[]{:S(2)}) copy-start(s32[8]{0:T(128)} %sources.3) | copy-start | bytes 100
  2.1 7.3 %collective-permute-start.5 = (bf16[4,16,1024]{2,1,0:T(8,128)(2,1)S(1)}, bf16[4,16,1024]{2,1,0:T(8,128)(2,1)S(1)}, u32[]{:S(2)}, u32[]{:S(2)}) collective-permute-start(bf16[4,16,1024]{2,1,0:T(8,128)(2,1)S(1)} %get-tuple-element.53), channel_id=1, source_target_pairs={{0,2},{2,0},{4,6},{6,4},{8,10},{10,8},{12,14},{14,12},{1,3},{3,1},... | collective-permute-start | bytes 393224 | tf_op jit(solution)/shard_map/ppermute | solution.py:414
  5.1 5.0 %collective-permute-start.6 = (bf16[4,16,1024]{2,1,0:T(8,128)(2,1)S(1)}, bf16[4,16,1024]{2,1,0:T(8,128)(2,1)S(1)}, u32[]{:S(2)}, u32[]{:S(2)}) collective-permute-start(bf16[4,16,1024]{2,1,0:T(8,128)(2,1)S(1)} %get-tuple-element.54), channel_id=1, source_target_pairs={{0,4},{2,6},{4,0},{6,2},{8,12},{10,14},{12,8},{14,10},{1,5},{3,7},... | collective-permute-start | bytes 393224 | tf_op jit(solution)/shard_map/ppermute | solution.py:414
  9.2 5.9 %collective-permute-start.7 = (bf16[4,16,1024]{2,1,0:T(8,128)(2,1)S(1)}, bf16[4,16,1024]{2,1,0:T(8,128)(2,1)S(1)}, u32[]{:S(2)}, u32[]{:S(2)}) collective-permute-start(bf16[4,16,1024]{2,1,0:T(8,128)(2,1)S(1)} %get-tuple-element.55), channel_id=1, source_target_pairs={{0,6},{2,4},{4,2},{6,0},{8,14},{10,12},{12,10},{14,8},{1,7},{3,5},... | collective-permute-start | bytes 393224 | tf_op jit(solution)/shard_map/ppermute | solution.py:414
  15.9 6.6 %collective-permute-start.12 = (bf16[6,8,1024]{2,1,0:T(8,128)(2,1)S(1)}, bf16[6,8,1024]{2,1,0:T(8,128)(2,1)S(1)}, u32[]{:S(2)}, u32[]{:S(2)}) collective-permute-start(bf16[6,8,1024]{2,1,0:T(8,128)(2,1)S(1)} %get-tuple-element.72), channel_id=1, source_target_pairs={{0,8},{2,10},{4,12},{6,14},{8,0},{10,2},{12,4},{14,6},{1,9},{3,11}... | collective-permute-start | bytes 294920 | tf_op jit(solution)/shard_map/ppermute | solution.py:414
  22.5 12.0 %copy-start.1 = (s32[16,64]{1,0:T(8,128)S(1)}, s32[16,64]{1,0:T(8,128)}, u32[]{:S(2)}) copy-start(s32[16,64]{1,0:T(8,128)} %valid.2) | copy-start | bytes 12292
  23.7 10.7 %collective-permute-start.15 = (bf16[64,1024]{1,0:T(8,128)(2,1)S(1)}, bf16[64,1024]{1,0:T(8,128)(2,1)S(1)}, u32[]{:S(2)}, u32[]{:S(2)}) collective-permute-start(bf16[64,1024]{1,0:T(8,128)(2,1)S(1)} %whiten.3.rest_0_), channel_id=1, source_target_pairs={{0,6},{2,4},{4,2},{6,0},{8,14},{10,12},{12,10},{14,8},{1,7},{3,5},... | collective-permute-start | bytes 393224 | tf_op jit(solution)/shard_map/ppermute | solution.py:414
  23.8 5.7 %collective-permute-start.8 = (bf16[6,8,1024]{2,1,0:T(8,128)(2,1)S(1)}, bf16[6,8,1024]{2,1,0:T(8,128)(2,1)S(1)}, u32[]{:S(2)}, u32[]{:S(2)}) collective-permute-start(bf16[6,8,1024]{2,1,0:T(8,128)(2,1)S(1)} %get-tuple-element.69), channel_id=1, source_target_pairs={{0,8},{2,10},{4,12},{6,14},{8,0},{10,2},{12,4},{14,6},{1,9},{3,11}... | collective-permute-start | bytes 294920 | tf_op jit(solution)/shard_map/ppermute | solution.py:414
  25.7 14.5 %collective-permute-start.14 = (bf16[64,1024]{1,0:T(8,128)(2,1)S(1)}, bf16[64,1024]{1,0:T(8,128)(2,1)S(1)}, u32[]{:S(2)}, u32[]{:S(2)}) collective-permute-start(bf16[64,1024]{1,0:T(8,128)(2,1)S(1)} %whiten.3.rest_0_), channel_id=1, source_target_pairs={{0,2},{2,0},{4,6},{6,4},{8,10},{10,8},{12,14},{14,12},{1,3},{3,1},... | collective-permute-start | bytes 393224 | tf_op jit(solution)/shard_map/ppermute | solution.py:414
  27.4 13.4 %collective-permute-start.13 = (bf16[64,1024]{1,0:T(8,128)(2,1)S(1)}, bf16[64,1024]{1,0:T(8,128)(2,1)S(1)}, u32[]{:S(2)}, u32[]{:S(2)}) collective-permute-start(bf16[64,1024]{1,0:T(8,128)(2,1)S(1)} %whiten.3.rest_0_), channel_id=1, source_target_pairs={{0,4},{2,6},{4,0},{6,2},{8,12},{10,14},{12,8},{14,10},{1,5},{3,7},... | collective-permute-start | bytes 393224 | tf_op jit(solution)/shard_map/ppermute | solution.py:414
  30.7 10.8 %collective-permute-start.11 = (bf16[64,1024]{1,0:T(8,128)(2,1)S(1)}, bf16[64,1024]{1,0:T(8,128)(2,1)S(1)}, u32[]{:S(2)}, u32[]{:S(2)}) collective-permute-start(bf16[64,1024]{1,0:T(8,128)(2,1)S(1)} %whiten.2.rest_0_), channel_id=1, source_target_pairs={{0,6},{2,4},{4,2},{6,0},{8,14},{10,12},{12,10},{14,8},{1,7},{3,5},... | collective-permute-start | bytes 393224 | tf_op jit(solution)/shard_map/ppermute | solution.py:414
  33.7 8.4 %collective-permute-start.10 = (bf16[64,1024]{1,0:T(8,128)(2,1)S(1)}, bf16[64,1024]{1,0:T(8,128)(2,1)S(1)}, u32[]{:S(2)}, u32[]{:S(2)}) collective-permute-start(bf16[64,1024]{1,0:T(8,128)(2,1)S(1)} %whiten.2.rest_0_), channel_id=1, source_target_pairs={{0,2},{2,0},{4,6},{6,4},{8,10},{10,8},{12,14},{14,12},{1,3},{3,1},... | collective-permute-start | bytes 393224 | tf_op jit(solution)/shard_map/ppermute | solution.py:414
  34.4 8.3 %collective-permute-start.9 = (bf16[64,1024]{1,0:T(8,128)(2,1)S(1)}, bf16[64,1024]{1,0:T(8,128)(2,1)S(1)}, u32[]{:S(2)}, u32[]{:S(2)}) collective-permute-start(bf16[64,1024]{1,0:T(8,128)(2,1)S(1)} %whiten.2.rest_0_), channel_id=1, source_target_pairs={{0,4},{2,6},{4,0},{6,2},{8,12},{10,14},{12,8},{14,10},{1,5},{3,7},... | collective-permute-start | bytes 393224 | tf_op jit(solution)/shard_map/ppermute | solution.py:414
  43.1 1.4 %collective-permute-start.16 = (bf16[16,8,512]{2,1,0:T(8,128)(2,1)S(1)}, bf16[16,8,512]{2,1,0:T(8,128)(2,1)S(1)}, u32[]{:S(2)}, u32[]{:S(2)}) collective-permute-start(bf16[16,8,512]{2,1,0:T(8,128)(2,1)S(1)} %shard_map.54), channel_id=1, source_target_pairs={{0,1},{1,0},{2,3},{3,2},{4,5},{5,4},{6,7},{7,6},{8,9},{9,8},{10,11... | collective-permute-start | bytes 393224 | tf_op jit(solution)/shard_map/ppermute | solution.py:473
